TPU v7x, 32 devices: a whole 2x2x4 slice. The times are simulated.
32 devices in a mesh: lon: 8 (over z, x), lat: 4 (over y, core).
Axes of the slice: x: 2, y: 2, z: 4, core: 2. Of those that a mesh axis runs over, the one named last changes fastest.
Arguments:
- field: float32 [2, 128, 512], P(None, 'lat', 'lon'), may hold values from -6 to 6
- gamma: float32 [2, 128, 512], P(None, 'lat', 'lon'), may hold values from 1 to 192
- kappa_zonal: float32 [2, 128, 512], P(None, 'lat', 'lon'), may hold values from 4096 to 49152
- kappa_merid: float32 [2, 128, 512], P(None, 'lat', 'lon'), may hold values from 1024 to 12288
- area: float32 [128, 512], P('lat', 'lon'), may hold values from 0.3 to 3
- sea_mask: int32 [128, 512], P('lat', 'lon'), may hold values from 0 to 1, as said below
- fold_pair: int32 [512], P('lon'), may hold values from 0 to 511, as said below
Outputs:
- covaried: float32 [2, 128, 512], P(None, 'lat', 'lon')
Inputs may be any that keep to these rules, and one draw needn't show every extreme that they name: `sea_mask`: ocean cells are 1 and land cells 0; land comes in rectangles, periodic in longitude. A mirror pairing across the fold: fold_pair[i] + i is the same odd number modulo 512 for every i, so fold_pair[fold_pair[i]] == i and fold_pair[i] != i.
All inputs are finite; a program needn't handle non-finite values.
Results may differ from a plain program's by a relative error of at most 0.00095.
Values sent between devices are 32-bit elements; how exact they have to be, the bound alone decides.
No kernel may reach another device: no remote copies, remote signals or barrier semaphores. Data moves between devices by JAX's collectives and lax.ppermute only.
A program may use at most 64 MiB of HBM per device.

v0:
```python
import jax
import jax.numpy as jnp
from jax import lax
from jax.sharding import PartitionSpec as P


def passed_along(block, axis, distance):
    devices = range(lax.axis_size(axis))
    route = [((i - distance) % len(devices), i) for i in devices]
    return lax.ppermute(block, axis, route)


def passed_along_2(value, axis, by):
    size = lax.axis_size(axis)
    pairs = [(i, i + by) for i in range(size) if 0 <= i + by < size]
    return lax.ppermute(value, axis, pairs)


def slide(values, offset, fill, wrap):
    if wrap:
        return jnp.roll(values, offset, axis=-1)
    edge = jnp.full(values.shape[:-1] + (abs(offset),), fill, values.dtype)
    if offset > 0:
        return jnp.concatenate([edge, values[..., :-offset]], axis=-1)
    return jnp.concatenate([values[..., -offset:], edge], axis=-1)


def reduce_lines(lower, diagonal, upper, source, wrap):
    length = source.shape[-1]
    stride = 1
    while stride < length:
        below_diag = slide(diagonal, stride, 1.0, wrap)
        above_diag = slide(diagonal, -stride, 1.0, wrap)
        factor_low = -lower / below_diag
        factor_up = -upper / above_diag
        new_diagonal = (
            diagonal
            + factor_low * slide(upper, stride, 0.0, wrap)
            + factor_up * slide(lower, -stride, 0.0, wrap)
        )
        source = (
            source
            + factor_low * slide(source, stride, 0.0, wrap)
            + factor_up * slide(source, -stride, 0.0, wrap)
        )
        lower = factor_low * slide(lower, stride, 0.0, wrap)
        upper = factor_up * slide(upper, -stride, 0.0, wrap)
        diagonal = new_diagonal
        stride = stride * 2
    if wrap:
        return source / (diagonal + lower + upper)
    return source / diagonal


def cyclic_solve(faces, source):
    before = jnp.roll(faces, 1, axis=-1)
    diagonal = 1.0 + before + faces
    return reduce_lines(-before, diagonal, -faces, source, True)


def open_solve(faces, source):
    before = jnp.concatenate([jnp.zeros_like(faces[..., :1]), faces[..., :-1]], axis=-1)
    diagonal = 1.0 + before + faces
    upper_band = jnp.concatenate([-faces[..., :-1], jnp.zeros_like(faces[..., :1])], axis=-1)
    return reduce_lines(-before, diagonal, upper_band, source, False)


def to_columns(blocks, lanes):
    levels, height, breadth = blocks.shape
    split = blocks.reshape(levels, height, lanes, breadth // lanes)
    return jnp.transpose(split, (2, 0, 3, 1))


def from_columns(pieces):
    lanes, levels, narrow, height = pieces.shape
    return jnp.transpose(pieces, (1, 3, 0, 2)).reshape(levels, height, lanes * narrow)


def local(field, gamma, kappa_zonal, kappa_merid, area, sea_mask, fold_pair):
    ocean_cells = sea_mask.astype(jnp.float32)
    east_edge = passed_along(ocean_cells[:, :1], "lon", -1)
    north_edge = passed_along_2(ocean_cells[:1, :], "lat", -1)
    east_ocean = jnp.concatenate([ocean_cells[:, 1:], east_edge], axis=1)
    north_ocean = jnp.concatenate([ocean_cells[1:], north_edge], axis=0)
    zonal_faces = kappa_zonal * (ocean_cells * east_ocean)[None]
    merid_faces = kappa_merid * (ocean_cells * north_ocean)[None]
    scaled = gamma * ocean_cells[None]
    lanes = lax.axis_size("lat")
    zonal_lines = lax.all_to_all(zonal_faces, "lon", split_axis=1, concat_axis=2, tiled=True)
    merid_lines = lax.all_to_all(
        to_columns(merid_faces, lanes), "lat", split_axis=0, concat_axis=3, tiled=True
    )[0]

    def zonal_pass(current):
        lines = lax.all_to_all(current, "lon", split_axis=1, concat_axis=2, tiled=True)
        return lax.all_to_all(
            cyclic_solve(zonal_lines, lines), "lon", split_axis=2, concat_axis=1, tiled=True
        )

    def merid_open(current):
        return lax.all_to_all(
            to_columns(current, lanes), "lat", split_axis=0, concat_axis=3, tiled=True
        )[0]

    def merid_close(columns):
        return from_columns(
            lax.all_to_all(columns[None], "lat", split_axis=3, concat_axis=0, tiled=True)
        )

    current = zonal_pass(scaled * field)
    columns = open_solve(merid_lines, merid_open(current))
    current = merid_close(columns)
    is_top = lax.axis_index("lat") == lanes - 1

    def fold_natural(values):
        top_cells = values[:, -1, :]
        whole_row = lax.all_gather(top_cells, "lon", axis=1, tiled=True)
        partner = jnp.take(whole_row, fold_pair, axis=1)
        return values.at[:, -1, :].set(jnp.where(is_top, 0.5 * (top_cells + partner), top_cells))

    current = fold_natural(current)
    current = current / area[None]
    current = fold_natural(current)
    current = merid_close(open_solve(merid_lines, merid_open(current)))
    current = zonal_pass(current)
    return scaled * current


def solution(mesh):
    return jax.shard_map(
        local,
        mesh=mesh,
        in_specs=(
            P(None, "lat", "lon"),
            P(None, "lat", "lon"),
            P(None, "lat", "lon"),
            P(None, "lat", "lon"),
            P("lat", "lon"),
            P("lat", "lon"),
            P("lon"),
        ),
        out_specs=P(None, "lat", "lon"),
        check_vma=False,
    )
```

profile of v0, /device:TPU:0, one launch (start us, length us, event | category | flops | bytes accessed | tf_op | source)
XLA Modules:
  0.0 188.0 jit_solution(8956095462419415965)
XLA Ops:
  0.0 0.7 convert_element_type.3
  0.7 1.4 collective-permute-start.1
  2.1 6.0 %collective-permute-start = (f32[32,1]{1,0:T(8,128)S(1)}, f32[32,1]{1,0:T(8,128)S(1)}, u32[]{:S(2)}, u32[]{:S(2)}) collective-permute-start(f32[32,1]{1,0:T(8,128)S(1)} %bitcast.116), channel_id=1, source_target_pairs={{4,0},{8,4},{12,8},{16,12},{20,16},{24,20},{28,24},{0,28},{5,1},{9... | collective-permute-start | bytes 392 | tf_op jit(solution)/shard_map/ppermute | solution.py:10
  8.3 0.7 copy-done
  9.0 0.7 reshape.122
  9.9 0.6 copy-done.1
  10.7 0.7 reshape.120
  11.4 3.5 %all-to-all-start.4 = ((f32[4,1,1024]{2,1,0:T(1,128)}), f32[4,1,1024]{2,1,0:T(1,128)S(1)}, u32[]{:S(2)}, u32[]{:S(2)}) async-start(f32[4,1,1024]{2,1,0:T(1,128)} %reshape.120), calls=%async_computation.4 | async-start | bytes 32768 | tf_op jit(solution)/shard_map/all_to_all | solution.py:90
  15.0 0.7 reshape.124
  15.7 3.1 %all-to-all-done.4 = f32[4,1,1024]{2,1,0:T(1,128)S(1)} async-done(((f32[4,1,1024]{2,1,0:T(1,128)}), f32[4,1,1024]{2,1,0:T(1,128)S(1)}, u32[]{:S(2)}, u32[]{:S(2)}) %all-to-all-start.4) | async-done | bytes 16416 | tf_op jit(solution)/shard_map/all_to_all | solution.py:90
  18.8 5.4 %all-to-all-start = ((f32[8,1,512]{2,1,0:T(1,128)}), f32[8,1,512]{2,1,0:T(1,128)S(1)}, u32[]{:S(2)}, u32[]{:S(2)}) async-start(f32[8,1,512]{2,1,0:T(1,128)} %reshape.122), calls=%async_computation | async-start | bytes 32768 | tf_op jit(solution)/shard_map/all_to_all | solution.py:95
  24.2 0.6 broadcast.223
  24.8 0.7 reduce.8
  25.8 4.9 %all-to-all-done = f32[8,1,512]{2,1,0:T(1,128)S(1)} async-done(((f32[8,1,512]{2,1,0:T(1,128)}), f32[8,1,512]{2,1,0:T(1,128)S(1)}, u32[]{:S(2)}, u32[]{:S(2)}) %all-to-all-start) | async-done | bytes 16416 | tf_op jit(solution)/shard_map/all_to_all | solution.py:95
  30.8 3.3 %all-to-all-start.1 = ((f32[8,1,512]{2,1,0:T(1,128)}), f32[8,1,512]{2,1,0:T(1,128)S(1)}, u32[]{:S(2)}, u32[]{:S(2)}) async-start(f32[8,1,512]{2,1,0:T(1,128)} %reshape.124), calls=%async_computation.1 | async-start | bytes 32768 | tf_op jit(solution)/shard_map/all_to_all | solution.py:89
  34.1 0.7 reduce.5
  35.2 5.4 %all-to-all-done.1 = f32[8,1,512]{2,1,0:T(1,128)S(1)} async-done(((f32[8,1,512]{2,1,0:T(1,128)}), f32[8,1,512]{2,1,0:T(1,128)S(1)}, u32[]{:S(2)}, u32[]{:S(2)}) %all-to-all-start.1) | async-done | bytes 16416 | tf_op jit(solution)/shard_map/all_to_all | solution.py:89
  40.6 0.7 reduce.4
  42.7 0.1 maximum_multiply_fusion.9
  47.9 0.3 copy.67
  48.2 1.3 reshape.126
  49.5 3.3 %all-to-all-start.2 = ((f32[8,1,512]{2,1,0:T(1,128)}), f32[8,1,512]{2,1,0:T(1,128)S(1)}, u32[]{:S(2)}, u32[]{:S(2)}) async-start(f32[8,1,512]{2,1,0:T(1,128)} %reshape.126), calls=%async_computation.2 | async-start | bytes 32768 | tf_op jit(solution)/shard_map/all_to_all | solution.py:96
  52.9 6.4 %all-to-all-done.2 = f32[8,1,512]{2,1,0:T(1,128)S(1)} async-done(((f32[8,1,512]{2,1,0:T(1,128)}), f32[8,1,512]{2,1,0:T(1,128)S(1)}, u32[]{:S(2)}, u32[]{:S(2)}) %all-to-all-start.2) | async-done | bytes 16416 | tf_op jit(solution)/shard_map/all_to_all | solution.py:96
  59.4 0.7 reduce.6
  60.1 0.8 reshape.127
  60.9 0.2 copy.68
  61.1 0.1 reshape.89
  61.4 0.7 reshape.128
  62.1 3.3 %all-to-all-start.3 = ((f32[4,1,1024]{2,1,0:T(1,128)}), f32[4,1,1024]{2,1,0:T(1,128)S(1)}, u32[]{:S(2)}, u32[]{:S(2)}) async-start(f32[4,1,1024]{2,1,0:T(1,128)} %reshape.128), calls=%async_computation.3 | async-start | bytes 32768 | tf_op jit(solution)/shard_map/all_to_all | solution.py:101
  65.4 3.7 %all-to-all-done.3 = f32[4,1,1024]{2,1,0:T(1,128)S(1)} async-done(((f32[4,1,1024]{2,1,0:T(1,128)}), f32[4,1,1024]{2,1,0:T(1,128)S(1)}, u32[]{:S(2)}, u32[]{:S(2)}) %all-to-all-start.3) | async-done | bytes 16416 | tf_op jit(solution)/shard_map/all_to_all | solution.py:101
  69.2 0.7 reduce.7
  73.2 0.1 copy.75
  73.3 0.8 reshape.130
  74.1 3.3 %all-to-all-start.5 = ((f32[4,1,1024]{2,1,0:T(1,128)}), f32[4,1,1024]{2,1,0:T(1,128)S(1)}, u32[]{:S(2)}, u32[]{:S(2)}) async-start(f32[4,1,1024]{2,1,0:T(1,128)} %reshape.130), calls=%async_computation.5 | async-start | bytes 32768 | tf_op jit(solution)/shard_map/all_to_all | solution.py:107
  77.4 3.8 %all-to-all-done.5 = f32[4,1,1024]{2,1,0:T(1,128)S(1)} async-done(((f32[4,1,1024]{2,1,0:T(1,128)}), f32[4,1,1024]{2,1,0:T(1,128)S(1)}, u32[]{:S(2)}, u32[]{:S(2)}) %all-to-all-start.5) | async-done | bytes 16416 | tf_op jit(solution)/shard_map/all_to_all | solution.py:107
  81.2 0.7 reduce.9
  81.9 0.2 reshape.131
  82.1 0.1 copy.98
  82.2 1.0 copy.77
  83.3 30.8 %all-gather = f32[2,1,512]{0,2,1:T(8,128)S(1)} all-gather(f32[2,1,64]{0,2,1:T(8,128)S(1)} %slice.1420), channel_id=2, replica_groups=mesh['lon'=8,'lat'=4] {'lon'}, dimensions={2}, use_global_device_ids=true | all-gather | bytes 4608 | tf_op jit(solution)/shard_map/all_gather | solution.py:117
  114.1 0.6 gather_fusion
  114.8 0.6 copy-done.5
  115.4 0.3 broadcast_divide_fusion
  115.7 30.7 %all-gather.1 = f32[2,1,512]{0,2,1:T(8,128)S(1)} all-gather(f32[2,1,64]{0,2,1:T(8,128)S(1)} %slice.1421), channel_id=3, replica_groups=mesh['lon'=8,'lat'=4] {'lon'}, dimensions={2}, use_global_device_ids=true | all-gather | bytes 4608 | tf_op jit(solution)/shard_map/all_gather | solution.py:117
  146.5 0.6 gather_fusion.1
  147.2 0.6 copy.88
  147.9 6.2 %all_to_all.168 = f32[4,1,1024]{2,1,0:T(1,128)S(1)} all-to-all(f32[4,1,1024]{2,1,0:T(1,128)S(1)} %reshape.132), channel_id=1, replica_groups=mesh['lon'=8,'lat'=4] {'lat'}, dimensions={0} | all-to-all | bytes 32768 | tf_op jit(solution)/shard_map/all_to_all | solution.py:101
  154.1 0.7 reduce.10
  156.1 0.1 divide_bitcast_fusion
  156.2 0.1 copy.90
  156.3 0.2 reshape.134
  156.5 6.2 %all_to_all.169 = f32[4,1,1024]{2,1,0:T(1,128)S(1)} all-to-all(f32[4,1,1024]{2,1,0:T(1,128)S(1)} %reshape.134), channel_id=1, replica_groups=mesh['lon'=8,'lat'=4] {'lat'}, dimensions={0} | all-to-all | bytes 32768 | tf_op jit(solution)/shard_map/all_to_all | solution.py:107
  162.7 0.7 reduce.11
  163.5 0.2 reshape.135
  163.9 0.1 reshape.136
  164.0 8.9 %all_to_all.170 = f32[8,1,512]{2,1,0:T(1,128)S(1)} all-to-all(f32[8,1,512]{2,1,0:T(1,128)S(1)} %reshape.136), channel_id=1, replica_groups=mesh['lon'=8,'lat'=4] {'lon'}, dimensions={0} | all-to-all | bytes 32768 | tf_op jit(solution)/shard_map/all_to_all | solution.py:95
  172.9 0.7 reduce.12
  175.6 0.3 copy.95
  175.9 0.7 reshape.138
  176.6 8.9 %all_to_all.171 = f32[8,1,512]{2,1,0:T(1,128)S(1)} all-to-all(f32[8,1,512]{2,1,0:T(1,128)S(1)} %reshape.138), channel_id=1, replica_groups=mesh['lon'=8,'lat'=4] {'lon'}, dimensions={0} | all-to-all | bytes 32768 | tf_op jit(solution)/shard_map/all_to_all | solution.py:96
  185.6 0.7 reduce.13
  186.3 0.8 reshape.139
  187.1 0.2 copy.103
  187.4 0.6 multiply_multiply_fusion
  (229 shorter events, 14.3 us)
Async XLA Ops:
  0.7 7.5 %copy-start.6 = (s32[64]{0:T(128)S(1)}, s32[64]{0:T(128)}, u32[]{:S(2)}) copy-start(s32[64]{0:T(128)} %param.19) | copy-start | bytes 772
  0.7 9.2 %collective-permute-start.1 = (f32[1,64]{1,0:T(1,128)S(1)}, f32[1,64]{1,0:T(1,128)S(1)}, u32[]{:S(2)}, u32[]{:S(2)}) collective-permute-start(f32[1,64]{1,0:T(1,128)S(1)} %slice.1367), channel_id=1, source_target_pairs={{1,0},{2,1},{3,2},{5,4},{6,5},{7,6},{9,8},{10,9},{11,10},{13,12},{... | collective-permute-start | bytes 776 | tf_op jit(solution)/shard_map/ppermute | solution.py:16
  2.1 7.7 %collective-permute-start = (f32[32,1]{1,0:T(8,128)S(1)}, f32[32,1]{1,0:T(8,128)S(1)}, u32[]{:S(2)}, u32[]{:S(2)}) collective-permute-start(f32[32,1]{1,0:T(8,128)S(1)} %bitcast.116), channel_id=1, source_target_pairs={{4,0},{8,4},{12,8},{16,12},{20,16},{24,20},{28,24},{0,28},{5,1},{9... | collective-permute-start | bytes 392 | tf_op jit(solution)/shard_map/ppermute | solution.py:10
  8.2 0.8 copy-start
  8.2 0.8 copy-start.2
  9.0 0.8 copy-start.3
  9.8 0.7 copy-start.1
  11.4 3.6 %copy-start.4 = (f32[2,32,64]{2,1,0:T(8,128)S(1)}, f32[2,32,64]{2,1,0:T(8,128)}, u32[]{:S(2)}) copy-start(f32[2,32,64]{2,1,0:T(8,128)} %param.15) | copy-start | bytes 49156
  11.4 7.4 %all-to-all-start.4 = ((f32[4,1,1024]{2,1,0:T(1,128)}), f32[4,1,1024]{2,1,0:T(1,128)S(1)}, u32[]{:S(2)}, u32[]{:S(2)}) async-start(f32[4,1,1024]{2,1,0:T(1,128)} %reshape.120), calls=%async_computation.4 | async-start | bytes 32768 | tf_op jit(solution)/shard_map/all_to_all | solution.py:90
  18.8 12.0 %all-to-all-start = ((f32[8,1,512]{2,1,0:T(1,128)}), f32[8,1,512]{2,1,0:T(1,128)S(1)}, u32[]{:S(2)}, u32[]{:S(2)}) async-start(f32[8,1,512]{2,1,0:T(1,128)} %reshape.122), calls=%async_computation | async-start | bytes 32768 | tf_op jit(solution)/shard_map/all_to_all | solution.py:95
  30.8 9.9 %all-to-all-start.1 = ((f32[8,1,512]{2,1,0:T(1,128)}), f32[8,1,512]{2,1,0:T(1,128)S(1)}, u32[]{:S(2)}, u32[]{:S(2)}) async-start(f32[8,1,512]{2,1,0:T(1,128)} %reshape.124), calls=%async_computation.1 | async-start | bytes 32768 | tf_op jit(solution)/shard_map/all_to_all | solution.py:89
  49.5 9.9 %all-to-all-start.2 = ((f32[8,1,512]{2,1,0:T(1,128)}), f32[8,1,512]{2,1,0:T(1,128)S(1)}, u32[]{:S(2)}, u32[]{:S(2)}) async-start(f32[8,1,512]{2,1,0:T(1,128)} %reshape.126), calls=%async_computation.2 | async-start | bytes 32768 | tf_op jit(solution)/shard_map/all_to_all | solution.py:96
  62.1 7.1 %all-to-all-start.3 = ((f32[4,1,1024]{2,1,0:T(1,128)}), f32[4,1,1024]{2,1,0:T(1,128)S(1)}, u32[]{:S(2)}, u32[]{:S(2)}) async-start(f32[4,1,1024]{2,1,0:T(1,128)} %reshape.128), calls=%async_computation.3 | async-start | bytes 32768 | tf_op jit(solution)/shard_map/all_to_all | solution.py:101
  74.1 7.1 %all-to-all-start.5 = ((f32[4,1,1024]{2,1,0:T(1,128)}), f32[4,1,1024]{2,1,0:T(1,128)S(1)}, u32[]{:S(2)}, u32[]{:S(2)}) async-start(f32[4,1,1024]{2,1,0:T(1,128)} %reshape.130), calls=%async_computation.5 | async-start | bytes 32768 | tf_op jit(solution)/shard_map/all_to_all | solution.py:107
  114.7 0.7 copy-start.5
where the time goes:
time: 189 us; the launch traced here: 188 us
  blocking collectives  91.9 us (49%)
  starting transfers between devices  29.6 us (16%)
  waiting for transfers between devices  27.5 us (15%)
  local copies, waits for them, and re-layouts  24.2 us (13%)
  other arithmetic  14 us (7%)
    all_gather x2, blocking collectives, fold_natural(): whole_row = lax.all_gather(top_cells, 'lon', axis=1, tiled=True)  61.6 us
    unnamed x35, local copies, waits for them, and re-layouts  10.7 us
    all_to_all x1, blocking collectives, zonal_pass(): lax.all_to_all(current, 'lon', split_axis=1, concat_axis=2, tiled=True)  8.94 us
    all_to_all x1, blocking collectives, zonal_pass(): lax.all_to_all(cyclic_solve(zonal_lines, lines), 'lon', split_axis=2, con...  8.94 us
    all_to_all x1, waiting for transfers between devices, zonal_pass(): lax.all_to_all(cyclic_solve(zonal_lines, lines), 'lon', split_axis=2, con...  6.44 us
    all_to_all x1, blocking collectives, merid_open(): lax.all_to_all(to_columns(current, lanes), 'lat', split_axis=0, concat_ax...  6.21 us
    all_to_all x1, blocking collectives, merid_close(): lax.all_to_all(columns[None], 'lat', split_axis=3, concat_axis=0, tiled=T...  6.21 us
    ppermute x1, starting transfers between devices, passed_along(): return lax.ppermute(block, axis, route)  6.03 us
  transfers between devices with their start and end apart: 8, of which 6 were waited for; matrix products, arithmetic and copies ran while one was open for 2% of the time, Pallas kernels for 0%

commit v1 on v0

--- a/solution.py
+++ b/solution.py
@@ -2,6 +2,27 @@
 import jax.numpy as jnp
 from jax import lax
 from jax.sharding import PartitionSpec as P
+
+
+def laid_out(parts, dim):
+    parts = jnp.moveaxis(parts, 0, dim)
+    shape = parts.shape
+    return parts.reshape(*shape[:dim], shape[dim] * shape[dim + 1], *shape[dim + 2 :])
+
+
+def doubled(array, axis):
+    size, position = (lax.axis_size(axis), lax.axis_index(axis))
+    tiles, distance = (array[None], 1)
+    while distance < size:
+        other = lax.ppermute(tiles, axis, [(i, i ^ distance) for i in range(size)])
+        low = position & distance == 0
+        tiles = jnp.concatenate([jnp.where(low, tiles, other), jnp.where(low, other, tiles)])
+        distance *= 2
+    return tiles
+
+
+def doubled_up(array, axis, dim):
+    return laid_out(doubled(array, axis), dim)
 
 
 def passed_along(block, axis, distance):
@@ -114,7 +135,7 @@
 
     def fold_natural(values):
         top_cells = values[:, -1, :]
-        whole_row = lax.all_gather(top_cells, "lon", axis=1, tiled=True)
+        whole_row = doubled_up(top_cells, "lon", 1)
         partner = jnp.take(whole_row, fold_pair, axis=1)
         return values.at[:, -1, :].set(jnp.where(is_top, 0.5 * (top_cells + partner), top_cells))
 

time: 189 us -> 151 us (0.80)
  blocking collectives: 91.9 us -> 30.3 us
  waiting for transfers between devices: 27.5 us -> 47.3 us
  starting transfers between devices: 29.6 us -> 33.7 us
    all_gather x2 -> x0, blocking collectives: 61.6 us -> none  [fold_natural(): whole_row = lax.all_gather(top_cells, 'lon', axis=1, tiled=True)]
    ppermute x0 -> x6, waiting for transfers between devices: none -> 19.2 us  [doubled(): other = lax.ppermute(tiles, axis, [(i, i ^ distance) for i in range(size)])]
    ppermute x0 -> x6, starting transfers between devices: none -> 3.46 us  [doubled(): other = lax.ppermute(tiles, axis, [(i, i ^ distance) for i in range(size)])]
    unnamed x35 -> x36, local copies, waits for them, and re-layouts: 10.7 us -> 9.05 us
  transfers between devices with their start and end apart: 8 -> 14, of which waited for: 6 -> 13; matrix products, arithmetic and copies ran while one was open for 2% -> 4% of each run, Pallas kernels for 0% -> 0%
where the time goes in v1:
time: 151 us; the launch traced here: 150 us
  waiting for transfers between devices  47.3 us (31%)
  starting transfers between devices  33.7 us (22%)
  blocking collectives  30.3 us (20%)
  local copies, waits for them, and re-layouts  24.2 us (16%)
  other arithmetic  13.2 us (9%)
    ppermute x6, waiting for transfers between devices, doubled(): other = lax.ppermute(tiles, axis, [(i, i ^ distance) for i in range(size)])  19.2 us
    unnamed x36, local copies, waits for them, and re-layouts  9.05 us
    all_to_all x1, blocking collectives, zonal_pass(): lax.all_to_all(current, 'lon', split_axis=1, concat_axis=2, tiled=True)  8.94 us
    all_to_all x1, blocking collectives, zonal_pass(): lax.all_to_all(cyclic_solve(zonal_lines, lines), 'lon', split_axis=2, con...  8.94 us
    all_to_all x1, waiting for transfers between devices, zonal_pass(): lax.all_to_all(cyclic_solve(zonal_lines, lines), 'lon', split_axis=2, con...  6.44 us
    all_to_all x1, blocking collectives, merid_close(): lax.all_to_all(columns[None], 'lat', split_axis=3, concat_axis=0, tiled=T...  6.21 us
    all_to_all x1, blocking collectives, merid_open(): lax.all_to_all(to_columns(current, lanes), 'lat', split_axis=0, concat_ax...  6.21 us
    all_to_all x1, starting transfers between devices, zonal_pass(): lax.all_to_all(current, 'lon', split_axis=1, concat_axis=2, tiled=True)  6.11 us
  transfers between devices with their start and end apart: 14, of which 13 were waited for; matrix products, arithmetic and copies ran while one was open for 4% of the time, Pallas kernels for 0%

profile of v1, /device:TPU:0, one launch (start us, length us, event | category | flops | bytes accessed | tf_op | source)
XLA Modules:
  0.0 149.5 jit_solution(2747146416814963600)
XLA Ops:
  0.0 0.7 convert_element_type.3
  0.7 1.3 collective-permute-start.1
  2.0 6.0 %collective-permute-start = (f32[32,1]{1,0:T(8,128)S(1)}, f32[32,1]{1,0:T(8,128)S(1)}, u32[]{:S(2)}, u32[]{:S(2)}) collective-permute-start(f32[32,1]{1,0:T(8,128)S(1)} %bitcast.127), channel_id=1, source_target_pairs={{4,0},{8,4},{12,8},{16,12},{20,16},{24,20},{28,24},{0,28},{5,1},{9... | collective-permute-start | bytes 392 | tf_op jit(solution)/shard_map/ppermute | solution.py:31
  8.2 0.7 reshape.130
  9.0 0.5 collective-permute-done
  9.9 0.7 reshape.128
  10.6 3.5 %all-to-all-start.4 = ((f32[4,1,1024]{2,1,0:T(1,128)}), f32[4,1,1024]{2,1,0:T(1,128)S(1)}, u32[]{:S(2)}, u32[]{:S(2)}) async-start(f32[4,1,1024]{2,1,0:T(1,128)} %reshape.128), calls=%async_computation.4 | async-start | bytes 32768 | tf_op jit(solution)/shard_map/all_to_all | solution.py:111
  14.1 0.7 reshape.132
  14.8 3.1 %all-to-all-done.4 = f32[4,1,1024]{2,1,0:T(1,128)S(1)} async-done(((f32[4,1,1024]{2,1,0:T(1,128)}), f32[4,1,1024]{2,1,0:T(1,128)S(1)}, u32[]{:S(2)}, u32[]{:S(2)}) %all-to-all-start.4) | async-done | bytes 16416 | tf_op jit(solution)/shard_map/all_to_all | solution.py:111
  18.0 6.1 %all-to-all-start = ((f32[8,1,512]{2,1,0:T(1,128)}), f32[8,1,512]{2,1,0:T(1,128)S(1)}, u32[]{:S(2)}, u32[]{:S(2)}) async-start(f32[8,1,512]{2,1,0:T(1,128)} %reshape.130), calls=%async_computation | async-start | bytes 32768 | tf_op jit(solution)/shard_map/all_to_all | solution.py:116
  24.1 0.5 broadcast.225
  24.6 0.7 reduce.12
  25.6 5.0 %all-to-all-done = f32[8,1,512]{2,1,0:T(1,128)S(1)} async-done(((f32[8,1,512]{2,1,0:T(1,128)}), f32[8,1,512]{2,1,0:T(1,128)S(1)}, u32[]{:S(2)}, u32[]{:S(2)}) %all-to-all-start) | async-done | bytes 16416 | tf_op jit(solution)/shard_map/all_to_all | solution.py:116
  30.7 3.3 %all-to-all-start.1 = ((f32[8,1,512]{2,1,0:T(1,128)}), f32[8,1,512]{2,1,0:T(1,128)S(1)}, u32[]{:S(2)}, u32[]{:S(2)}) async-start(f32[8,1,512]{2,1,0:T(1,128)} %reshape.132), calls=%async_computation.1 | async-start | bytes 32768 | tf_op jit(solution)/shard_map/all_to_all | solution.py:110
  34.0 0.7 reduce.9
  35.0 5.5 %all-to-all-done.1 = f32[8,1,512]{2,1,0:T(1,128)S(1)} async-done(((f32[8,1,512]{2,1,0:T(1,128)}), f32[8,1,512]{2,1,0:T(1,128)S(1)}, u32[]{:S(2)}, u32[]{:S(2)}) %all-to-all-start.1) | async-done | bytes 16416 | tf_op jit(solution)/shard_map/all_to_all | solution.py:110
  40.5 0.7 reduce.8
  47.7 0.3 copy.67
  48.0 1.3 reshape.134
  49.3 3.3 %all-to-all-start.2 = ((f32[8,1,512]{2,1,0:T(1,128)}), f32[8,1,512]{2,1,0:T(1,128)S(1)}, u32[]{:S(2)}, u32[]{:S(2)}) async-start(f32[8,1,512]{2,1,0:T(1,128)} %reshape.134), calls=%async_computation.2 | async-start | bytes 32768 | tf_op jit(solution)/shard_map/all_to_all | solution.py:117
  52.7 6.4 %all-to-all-done.2 = f32[8,1,512]{2,1,0:T(1,128)S(1)} async-done(((f32[8,1,512]{2,1,0:T(1,128)}), f32[8,1,512]{2,1,0:T(1,128)S(1)}, u32[]{:S(2)}, u32[]{:S(2)}) %all-to-all-start.2) | async-done | bytes 16416 | tf_op jit(solution)/shard_map/all_to_all | solution.py:117
  59.2 0.7 reduce.10
  59.9 0.8 reshape.135
  60.7 0.2 copy.68
  61.1 0.7 reshape.136
  61.9 3.3 %all-to-all-start.3 = ((f32[4,1,1024]{2,1,0:T(1,128)}), f32[4,1,1024]{2,1,0:T(1,128)S(1)}, u32[]{:S(2)}, u32[]{:S(2)}) async-start(f32[4,1,1024]{2,1,0:T(1,128)} %reshape.136), calls=%async_computation.3 | async-start | bytes 32768 | tf_op jit(solution)/shard_map/all_to_all | solution.py:122
  65.2 3.7 %all-to-all-done.3 = f32[4,1,1024]{2,1,0:T(1,128)S(1)} async-done(((f32[4,1,1024]{2,1,0:T(1,128)}), f32[4,1,1024]{2,1,0:T(1,128)S(1)}, u32[]{:S(2)}, u32[]{:S(2)}) %all-to-all-start.3) | async-done | bytes 16416 | tf_op jit(solution)/shard_map/all_to_all | solution.py:122
  68.9 0.7 reduce.11
  73.0 0.8 reshape.138
  73.8 3.4 %all-to-all-start.5 = ((f32[4,1,1024]{2,1,0:T(1,128)}), f32[4,1,1024]{2,1,0:T(1,128)S(1)}, u32[]{:S(2)}, u32[]{:S(2)}) async-start(f32[4,1,1024]{2,1,0:T(1,128)} %reshape.138), calls=%async_computation.5 | async-start | bytes 32768 | tf_op jit(solution)/shard_map/all_to_all | solution.py:128
  77.2 3.8 %all-to-all-done.5 = f32[4,1,1024]{2,1,0:T(1,128)S(1)} async-done(((f32[4,1,1024]{2,1,0:T(1,128)}), f32[4,1,1024]{2,1,0:T(1,128)S(1)}, u32[]{:S(2)}, u32[]{:S(2)}) %all-to-all-start.5) | async-done | bytes 16416 | tf_op jit(solution)/shard_map/all_to_all | solution.py:128
  81.0 0.7 reduce.13
  82.2 0.6 collective-permute-start.2
  82.8 3.0 %collective-permute-done.2 = f32[1,2,64]{2,1,0:T(2,128)S(1)} collective-permute-done((f32[1,2,64]{2,1,0:T(2,128)S(1)}, f32[1,2,64]{2,1,0:T(2,128)S(1)}, u32[]{:S(2)}, u32[]{:S(2)}) %collective-permute-start.2) | collective-permute-done | bytes 544 | tf_op jit(solution)/shard_map/ppermute | solution.py:17
  85.9 0.5 collective-permute-start.3
  86.4 3.1 %collective-permute-done.3 = f32[2,2,64]{2,1,0:T(2,128)S(1)} collective-permute-done((f32[2,2,64]{2,1,0:T(2,128)S(1)}, f32[2,2,64]{2,1,0:T(2,128)S(1)}, u32[]{:S(2)}, u32[]{:S(2)}) %collective-permute-start.3) | collective-permute-done | bytes 1056 | tf_op jit(solution)/shard_map/ppermute | solution.py:17
  89.5 0.6 collective-permute-start.4
  90.2 0.5 copy.100
  90.7 3.4 %collective-permute-done.4 = f32[4,2,64]{2,1,0:T(2,128)S(1)} collective-permute-done((f32[4,2,64]{2,1,0:T(2,128)S(1)}, f32[4,2,64]{2,1,0:T(2,128)S(1)}, u32[]{:S(2)}, u32[]{:S(2)}) %collective-permute-start.4) | collective-permute-done | bytes 2080 | tf_op jit(solution)/shard_map/ppermute | solution.py:17
  94.3 0.6 gather_fusion
  95.0 0.5 copy.82
  95.5 0.3 scatter.6
  96.0 0.6 collective-permute-start.5
  96.6 3.0 %collective-permute-done.5 = f32[1,2,64]{2,1,0:T(2,128)S(1)} collective-permute-done((f32[1,2,64]{2,1,0:T(2,128)S(1)}, f32[1,2,64]{2,1,0:T(2,128)S(1)}, u32[]{:S(2)}, u32[]{:S(2)}) %collective-permute-start.5) | collective-permute-done | bytes 544 | tf_op jit(solution)/shard_map/ppermute | solution.py:17
  99.6 0.5 collective-permute-start.6
  100.2 3.1 %collective-permute-done.6 = f32[2,2,64]{2,1,0:T(2,128)S(1)} collective-permute-done((f32[2,2,64]{2,1,0:T(2,128)S(1)}, f32[2,2,64]{2,1,0:T(2,128)S(1)}, u32[]{:S(2)}, u32[]{:S(2)}) %collective-permute-start.6) | collective-permute-done | bytes 1056 | tf_op jit(solution)/shard_map/ppermute | solution.py:17
  103.3 0.6 collective-permute-start.7
  103.9 0.5 copy.103
  104.4 3.5 %collective-permute-done.7 = f32[4,2,64]{2,1,0:T(2,128)S(1)} collective-permute-done((f32[4,2,64]{2,1,0:T(2,128)S(1)}, f32[4,2,64]{2,1,0:T(2,128)S(1)}, u32[]{:S(2)}, u32[]{:S(2)}) %collective-permute-start.7) | collective-permute-done | bytes 2080 | tf_op jit(solution)/shard_map/ppermute | solution.py:17
  108.0 0.6 gather_fusion.1
  108.7 0.5 copy.88
  109.2 0.3 scatter.9
  109.7 6.2 %all_to_all.168 = f32[4,1,1024]{2,1,0:T(1,128)S(1)} all-to-all(f32[4,1,1024]{2,1,0:T(1,128)S(1)} %reshape.140), channel_id=1, replica_groups=mesh['lon'=8,'lat'=4] {'lat'}, dimensions={0} | all-to-all | bytes 32768 | tf_op jit(solution)/shard_map/all_to_all | solution.py:122
  115.9 0.7 reduce.14
  118.2 6.2 %all_to_all.169 = f32[4,1,1024]{2,1,0:T(1,128)S(1)} all-to-all(f32[4,1,1024]{2,1,0:T(1,128)S(1)} %reshape.142), channel_id=1, replica_groups=mesh['lon'=8,'lat'=4] {'lat'}, dimensions={0} | all-to-all | bytes 32768 | tf_op jit(solution)/shard_map/all_to_all | solution.py:128
  124.4 0.7 reduce.15
  125.6 8.9 %all_to_all.170 = f32[8,1,512]{2,1,0:T(1,128)S(1)} all-to-all(f32[8,1,512]{2,1,0:T(1,128)S(1)} %reshape.144), channel_id=1, replica_groups=mesh['lon'=8,'lat'=4] {'lon'}, dimensions={0} | all-to-all | bytes 32768 | tf_op jit(solution)/shard_map/all_to_all | solution.py:116
  134.6 0.7 reduce.16
  137.2 0.3 copy.96
  137.5 0.7 reshape.146
  138.2 8.9 %all_to_all.171 = f32[8,1,512]{2,1,0:T(1,128)S(1)} all-to-all(f32[8,1,512]{2,1,0:T(1,128)S(1)} %reshape.146), channel_id=1, replica_groups=mesh['lon'=8,'lat'=4] {'lon'}, dimensions={0} | all-to-all | bytes 32768 | tf_op jit(solution)/shard_map/all_to_all | solution.py:117
  147.2 0.7 reduce.17
  147.9 0.8 reshape.147
  148.9 0.6 multiply_multiply_fusion
  (260 shorter events, 16.9 us)
Async XLA Ops:
  0.7 8.8 %collective-permute-start.1 = (f32[1,64]{1,0:T(1,128)S(1)}, f32[1,64]{1,0:T(1,128)S(1)}, u32[]{:S(2)}, u32[]{:S(2)}) collective-permute-start(f32[1,64]{1,0:T(1,128)S(1)} %slice.1367), channel_id=1, source_target_pairs={{1,0},{2,1},{3,2},{5,4},{6,5},{7,6},{9,8},{10,9},{11,10},{13,12},{... | collective-permute-start | bytes 776 | tf_op jit(solution)/shard_map/ppermute | solution.py:37
  2.0 6.1 %copy-start = (f32[2,32,64]{2,1,0:T(8,128)S(1)}, f32[2,32,64]{2,1,0:T(8,128)}, u32[]{:S(2)}) copy-start(f32[2,32,64]{2,1,0:T(8,128)} %param.14) | copy-start | bytes 49156
  2.0 6.1 %copy-start.2 = (f32[2,32,64]{2,1,0:T(8,128)S(1)}, f32[2,32,64]{2,1,0:T(8,128)}, u32[]{:S(2)}) copy-start(f32[2,32,64]{2,1,0:T(8,128)} %param.13) | copy-start | bytes 49156
  2.0 7.5 %collective-permute-start = (f32[32,1]{1,0:T(8,128)S(1)}, f32[32,1]{1,0:T(8,128)S(1)}, u32[]{:S(2)}, u32[]{:S(2)}) collective-permute-start(f32[32,1]{1,0:T(8,128)S(1)} %bitcast.127), channel_id=1, source_target_pairs={{4,0},{8,4},{12,8},{16,12},{20,16},{24,20},{28,24},{0,28},{5,1},{9... | collective-permute-start | bytes 392 | tf_op jit(solution)/shard_map/ppermute | solution.py:31
  8.2 0.8 copy-start.3
  9.0 0.7 copy-start.1
  10.6 3.6 %copy-start.4 = (f32[2,32,64]{2,1,0:T(8,128)S(1)}, f32[2,32,64]{2,1,0:T(8,128)}, u32[]{:S(2)}) copy-start(f32[2,32,64]{2,1,0:T(8,128)} %param.15) | copy-start | bytes 49156
  10.6 7.4 %all-to-all-start.4 = ((f32[4,1,1024]{2,1,0:T(1,128)}), f32[4,1,1024]{2,1,0:T(1,128)S(1)}, u32[]{:S(2)}, u32[]{:S(2)}) async-start(f32[4,1,1024]{2,1,0:T(1,128)} %reshape.128), calls=%async_computation.4 | async-start | bytes 32768 | tf_op jit(solution)/shard_map/all_to_all | solution.py:111
  18.0 12.7 %all-to-all-start = ((f32[8,1,512]{2,1,0:T(1,128)}), f32[8,1,512]{2,1,0:T(1,128)S(1)}, u32[]{:S(2)}, u32[]{:S(2)}) async-start(f32[8,1,512]{2,1,0:T(1,128)} %reshape.130), calls=%async_computation | async-start | bytes 32768 | tf_op jit(solution)/shard_map/all_to_all | solution.py:116
  30.7 9.9 %all-to-all-start.1 = ((f32[8,1,512]{2,1,0:T(1,128)}), f32[8,1,512]{2,1,0:T(1,128)S(1)}, u32[]{:S(2)}, u32[]{:S(2)}) async-start(f32[8,1,512]{2,1,0:T(1,128)} %reshape.132), calls=%async_computation.1 | async-start | bytes 32768 | tf_op jit(solution)/shard_map/all_to_all | solution.py:110
  49.3 9.9 %all-to-all-start.2 = ((f32[8,1,512]{2,1,0:T(1,128)}), f32[8,1,512]{2,1,0:T(1,128)S(1)}, u32[]{:S(2)}, u32[]{:S(2)}) async-start(f32[8,1,512]{2,1,0:T(1,128)} %reshape.134), calls=%async_computation.2 | async-start | bytes 32768 | tf_op jit(solution)/shard_map/all_to_all | solution.py:117
  61.9 7.1 %all-to-all-start.3 = ((f32[4,1,1024]{2,1,0:T(1,128)}), f32[4,1,1024]{2,1,0:T(1,128)S(1)}, u32[]{:S(2)}, u32[]{:S(2)}) async-start(f32[4,1,1024]{2,1,0:T(1,128)} %reshape.136), calls=%async_computation.3 | async-start | bytes 32768 | tf_op jit(solution)/shard_map/all_to_all | solution.py:122
  73.8 3.4 %copy-start.6 = (s32[64]{0:T(128)S(1)}, s32[64]{0:T(128)}, u32[]{:S(2)}) copy-start(s32[64]{0:T(128)} %param.19) | copy-start | bytes 772
  73.8 7.2 %all-to-all-start.5 = ((f32[4,1,1024]{2,1,0:T(1,128)}), f32[4,1,1024]{2,1,0:T(1,128)S(1)}, u32[]{:S(2)}, u32[]{:S(2)}) async-start(f32[4,1,1024]{2,1,0:T(1,128)} %reshape.138), calls=%async_computation.5 | async-start | bytes 32768 | tf_op jit(solution)/shard_map/all_to_all | solution.py:128
  82.2 3.6 %collective-permute-start.2 = (f32[1,2,64]{2,1,0:T(2,128)S(1)}, f32[1,2,64]{2,1,0:T(2,128)S(1)}, u32[]{:S(2)}, u32[]{:S(2)}) collective-permute-start(f32[1,2,64]{2,1,0:T(2,128)S(1)} %bitcast.149), channel_id=1, source_target_pairs={{0,4},{4,0},{8,12},{12,8},{16,20},{20,16},{24,28},{28,24},{1,5},{5... | collective-permute-start | bytes 1544 | tf_op jit(solution)/shard_map/ppermute | solution.py:17
  85.9 3.6 %collective-permute-start.3 = (f32[2,2,64]{2,1,0:T(2,128)S(1)}, f32[2,2,64]{2,1,0:T(2,128)S(1)}, u32[]{:S(2)}, u32[]{:S(2)}) collective-permute-start(f32[2,2,64]{2,1,0:T(2,128)S(1)} %pad_maximum_fusion.8), channel_id=1, source_target_pairs={{0,8},{4,12},{8,0},{12,4},{16,24},{20,28},{24,16},{28,20},{1,9},{5... | collective-permute-start | bytes 3080 | tf_op jit(solution)/shard_map/ppermute | solution.py:17
  86.4 3.7 %copy-start.5 = (f32[32,64]{1,0:T(8,128)S(1)}, f32[32,64]{1,0:T(8,128)}, u32[]{:S(2)}) copy-start(f32[32,64]{1,0:T(8,128)} %param.17) | copy-start | bytes 24580
  89.5 4.6 %collective-permute-start.4 = (f32[4,2,64]{2,1,0:T(2,128)S(1)}, f32[4,2,64]{2,1,0:T(2,128)S(1)}, u32[]{:S(2)}, u32[]{:S(2)}) collective-permute-start(f32[4,2,64]{2,1,0:T(2,128)S(1)} %pad_maximum_fusion.6), channel_id=1, source_target_pairs={{0,16},{4,20},{8,24},{12,28},{16,0},{20,4},{24,8},{28,12},{1,17},{... | collective-permute-start | bytes 6152 | tf_op jit(solution)/shard_map/ppermute | solution.py:17
  96.0 3.6 %collective-permute-start.5 = (f32[1,2,64]{2,1,0:T(2,128)S(1)}, f32[1,2,64]{2,1,0:T(2,128)S(1)}, u32[]{:S(2)}, u32[]{:S(2)}) collective-permute-start(f32[1,2,64]{2,1,0:T(2,128)S(1)} %bitcast.150), channel_id=1, source_target_pairs={{0,4},{4,0},{8,12},{12,8},{16,20},{20,16},{24,28},{28,24},{1,5},{5... | collective-permute-start | bytes 1544 | tf_op jit(solution)/shard_map/ppermute | solution.py:17
  99.6 3.6 %collective-permute-start.6 = (f32[2,2,64]{2,1,0:T(2,128)S(1)}, f32[2,2,64]{2,1,0:T(2,128)S(1)}, u32[]{:S(2)}, u32[]{:S(2)}) collective-permute-start(f32[2,2,64]{2,1,0:T(2,128)S(1)} %pad_maximum_fusion.9), channel_id=1, source_target_pairs={{0,8},{4,12},{8,0},{12,4},{16,24},{20,28},{24,16},{28,20},{1,9},{5... | collective-permute-start | bytes 3080 | tf_op jit(solution)/shard_map/ppermute | solution.py:17
  103.3 4.6 %collective-permute-start.7 = (f32[4,2,64]{2,1,0:T(2,128)S(1)}, f32[4,2,64]{2,1,0:T(2,128)S(1)}, u32[]{:S(2)}, u32[]{:S(2)}) collective-permute-start(f32[4,2,64]{2,1,0:T(2,128)S(1)} %pad_maximum_fusion.7), channel_id=1, source_target_pairs={{0,16},{4,20},{8,24},{12,28},{16,0},{20,4},{24,8},{28,12},{1,17},{... | collective-permute-start | bytes 6152 | tf_op jit(solution)/shard_map/ppermute | solution.py:17
